TPU v7x, 256 devices: a whole 4x4x8 slice. The times are simulated.
256 devices in a mesh: row: 16 (over y, x), col: 2 (over core), ctx: 8 (over z).
Axes of the slice: x: 4, y: 4, z: 8, core: 2. Of those that a mesh axis runs over, the one named last changes fastest.
Arguments:
- queries: bfloat16 [8192, 6144], P(('col', 'ctx'), 'row'), may hold values from -16 to 16
- keys: bfloat16 [8192, 6144], P(('col', 'ctx'), 'row'), may hold values from -16 to 16
- values: bfloat16 [8192, 6144], P(('col', 'ctx'), 'row'), may hold values from -6 to 6
- out_weight: bfloat16 [6144, 6144], P('col', 'row'), may hold values from -0.078125 to 0.078125
- cotangent: bfloat16 [8192, 6144], P(('col', 'ctx'), 'row'), may hold values from -0.125 to 0.125
- block_mask: int32 [16, 16], replicated, may hold values from 0 to 1, as said below
Outputs:
- mixed_out: bfloat16 [8192, 6144], P(('col', 'ctx'), 'row')
- grad_weight: bfloat16 [6144, 6144], P(('col', 'ctx'), 'row')
Inputs may be any that keep to these rules, and one draw needn't show every extreme that they name: block_mask[i, i] is 1 for every block i, and block_mask[i, j] is 0 for j > i.
All inputs are finite; a program needn't handle non-finite values.
Results may differ from a plain program's by a relative error of at most 0.013.
Values may be sent and summed in bfloat16 or wider, within the bound.
A program may use at most 64 MiB of HBM per device.

v0:
```python
import math
import jax
import jax.numpy as jnp
from jax import lax
from jax.sharding import PartitionSpec as P

HD = 128
BLOCK = 512
NEGATIVE_FILL = -1e30


def attend_block(carried, query_heads, key_block, value_block, allowed, score_scale):
    run_max, run_sum, weighted = carried
    tok_rows, head_count, head_size = query_heads.shape
    key_heads = key_block.reshape(key_block.shape[0], head_count, head_size)
    value_heads = value_block.reshape(value_block.shape[0], head_count, head_size)
    scores = (
        jnp.einsum("thd,uhd->thu", query_heads, key_heads, preferred_element_type=jnp.float32)
        * score_scale
    )
    scores = jnp.where(allowed[:, None, None], scores, NEGATIVE_FILL)
    new_max = jnp.maximum(run_max, jnp.max(scores, axis=2))
    correction = jnp.exp(run_max - new_max)
    weights = jnp.where(allowed[:, None, None], jnp.exp(scores - new_max[:, :, None]), 0.0)
    new_sum = run_sum * correction + jnp.sum(weights, axis=2)
    product = jnp.einsum(
        "thu,uhd->thd",
        weights.astype(jnp.bfloat16),
        value_heads,
        preferred_element_type=jnp.float32,
    )
    new_weighted = weighted * correction[:, :, None] + product
    return (new_max, new_sum, new_weighted)


def body(queries, keys, values, out_weight, cotangent, block_mask):
    tok_rows, feature_width = queries.shape
    head_count = feature_width // HD
    query_heads = queries.reshape(tok_rows, head_count, HD)
    score_scale = 1.0 / math.sqrt(HD)
    local_blocks = tok_rows // BLOCK
    first_block = lax.axis_index(("col", "ctx")) * local_blocks
    local_mask = lax.dynamic_slice_in_dim(block_mask, first_block, local_blocks, 0)
    start_state = (
        jnp.full((tok_rows, head_count), NEGATIVE_FILL, jnp.float32),
        jnp.zeros((tok_rows, head_count), jnp.float32),
        jnp.zeros((tok_rows, head_count, HD), jnp.float32),
    )
    key_piece = lax.all_gather(keys, ("col", "ctx"), axis=0, tiled=True)
    value_piece = lax.all_gather(values, ("col", "ctx"), axis=0, tiled=True)
    block_count = key_piece.shape[0] // BLOCK
    key_stack = key_piece.reshape(block_count, BLOCK, feature_width)
    value_stack = value_piece.reshape(block_count, BLOCK, feature_width)
    block_columns = jnp.arange(block_count, dtype=jnp.int32)

    def one_block(state_in, entries):
        key_block, value_block, block_column = entries
        mask_column = lax.dynamic_index_in_dim(local_mask, block_column, 1, keepdims=False)
        allowed = jnp.repeat(mask_column, BLOCK, total_repeat_length=tok_rows) == 1
        updated = attend_block(state_in, query_heads, key_block, value_block, allowed, score_scale)
        return (updated, None)

    state_out, _ = lax.scan(one_block, start_state, (key_stack, value_stack, block_columns))
    run_max, run_sum, weighted = state_out
    attended = (
        (weighted / run_sum[:, :, None]).reshape(tok_rows, feature_width).astype(jnp.bfloat16)
    )
    all_heads = lax.all_gather(attended, "row", axis=1, tiled=True)
    head_columns = all_heads
    mixed_out = jnp.dot(
        head_columns,
        lax.all_gather(out_weight, "col", axis=0, tiled=True),
        preferred_element_type=jnp.float32,
    )
    head_columns = all_heads
    grad_weight = lax.psum_scatter(
        lax.dot_general(
            head_columns, cotangent, (((0,), (0,)), ((), ())), preferred_element_type=jnp.float32
        ),
        ("col", "ctx"),
        scatter_dimension=0,
        tiled=True,
    )
    return (mixed_out.astype(jnp.bfloat16), grad_weight.astype(jnp.bfloat16))


def solution(mesh):
    in_specs = (
        P(("col", "ctx"), "row"),
        P(("col", "ctx"), "row"),
        P(("col", "ctx"), "row"),
        P("col", "row"),
        P(("col", "ctx"), "row"),
        P(),
    )
    out_specs = (P(("col", "ctx"), "row"), P(("col", "ctx"), "row"))
    return jax.shard_map(body, mesh=mesh, in_specs=in_specs, out_specs=out_specs, check_vma=False)
```

profile of v0, /device:TPU:1, one launch (start us, length us, event | category | flops | bytes accessed | tf_op | source)
XLA Modules:
  0.0 622.6 jit_solution(9049366893125646251)
XLA Ops:
  12.0 48.1 %all-gather.5.cloned.1.call-done = bf16[8192,384]{1,0:T(8,128)(2,1)} async-done(((bf16[512,384]{1,0:T(8,128)(2,1)}), bf16[8192,384]{1,0:T(8,128)(2,1)}) %all-gather.5.cloned.1.call-update) | async-done | bytes 6291472 | tf_op jit(solution)/shard_map/all_gather | solution.py:49
  60.1 46.5 %all-gather.7.cloned.1.call-done = bf16[8192,384]{1,0:T(8,128)(2,1)} async-done(((bf16[512,384]{1,0:T(8,128)(2,1)}), bf16[8192,384]{1,0:T(8,128)(2,1)}) %all-gather.7.cloned.1.call-update) | async-done | bytes 6291472 | tf_op jit(solution)/shard_map/all_gather | solution.py:50
  107.2 304.6 %while.22 = (s32[]{:T(128)}, f32[512,3]{0,1:T(4,128)}, f32[512,3]{0,1:T(4,128)}, f32[512,3,128]{0,2,1:T(8,128)}, s32[16]{0:T(128)}, /*index=5*/s32[1,16]{1,0:T(1...) while((s32[]{:T(128)}, f32[512,3]{0,1:T(4,128)}, ...), condition=%wide.region_3.4_spmd.clone, body=%wide.region_0.3_spmd.clone.sunk | while | flops 413474304 | bytes 15433919 | solution.py:63
  114.3 2.4 bitcast_reduce_fusion.2
  120.7 3.4 fusion.42
  131.8 2.4 bitcast_reduce_fusion.2
  139.5 3.7 fusion.42
  151.0 2.4 bitcast_reduce_fusion.2
  158.7 3.7 fusion.42
  177.8 3.7 fusion.42
  189.2 2.4 bitcast_reduce_fusion.2
  197.0 3.7 fusion.42
  208.4 2.4 bitcast_reduce_fusion.2
  216.1 3.7 fusion.42
  235.2 3.7 fusion.42
  254.4 3.7 fusion.42
  265.8 2.4 bitcast_reduce_fusion.2
  273.5 3.7 fusion.42
  292.7 3.7 fusion.42
  311.8 3.7 fusion.42
  323.2 2.4 bitcast_reduce_fusion.2
  330.9 3.7 fusion.42
  350.1 3.7 fusion.42
  361.5 2.4 bitcast_reduce_fusion.2
  369.2 3.7 fusion.42
  388.3 3.7 fusion.42
  407.5 3.7 fusion.42
  414.4 64.1 %all-gather.9.cloned.1.call-done = bf16[512,6144]{0,1:T(8,128)(2,1)} async-done(((bf16[512,384]{0,1:T(8,128)(2,1)}), bf16[512,6144]{0,1:T(8,128)(2,1)}) %all-gather.9.cloned.1.call-update) | async-done | bytes 6291472 | tf_op jit(solution)/shard_map/all_gather | solution.py:68
  478.5 9.9 %fusion.19 = f32[6144,384]{1,0:T(8,128)} fusion(bf16[512,6144]{0,1:T(8,128)(2,1)} %all-gather.9.cloned.1.call-done, bf16[512,384]{1,0:T(8,128)(2,1)S(1)} %copy-done), kind=kOutput, calls=%fused_computation.27 | convolution fusion | flops 2415919104 | bytes 16121856 | tf_op jit(solution)/shard_map/dot_general | solution.py:77
  488.4 12.0 %all-gather.11.cloned.1.call-done = bf16[6144,384]{1,0:T(8,128)(2,1)} async-done(((bf16[3072,384]{1,0:T(8,128)(2,1)}), bf16[6144,384]{1,0:T(8,128)(2,1)}) %all-gather.11.cloned.1.call-update) | async-done | bytes 4718608 | tf_op jit(solution)/shard_map/all_gather | solution.py:72
  500.4 8.3 %convolution_convert_fusion = bf16[512,384]{1,0:T(8,128)(2,1)} fusion(bf16[512,6144]{0,1:T(8,128)(2,1)} %all-gather.9.cloned.1.call-done, bf16[6144,384]{1,0:T(8,128)(2,1)} %all-gather.11.cloned.1.call-done), kind=kOutput, calls=%fused_computation.23 | convolution fusion | flops 2416115712 | bytes 11403264 | tf_op jit(solution)/shard_map/dot_general | solution.py:70
  508.7 105.5 %reduce-scatter.2.cloned.1.call-done = f32[384,384]{1,0:T(8,128)} async-done(((f32[6144,384]{1,0:T(8,128)}), f32[384,384]{1,0:T(8,128)}) %reduce-scatter.2.cloned.1.call-update) | async-done | bytes 589840 | tf_op jit(solution)/shard_map/reduce_scatter | solution.py:76
  (173 shorter events, 206.9 us)
Async XLA Ops:
  7.2 471.3 %copy-start = (bf16[512,384]{1,0:T(8,128)(2,1)S(1)}, bf16[512,384]{1,0:T(8,128)(2,1)}, u32[]{:S(2)}) copy-start(bf16[512,384]{1,0:T(8,128)(2,1)} %param.16) | copy-start | bytes 1179652
  7.2 53.0 %all-gather.5.cloned.1.call-start = ((), (), s32[]{:S(2)}) async-start(), calls=%async_computation.1 | async-start | bytes 6684672 | tf_op jit(solution)/shard_map/all_gather | solution.py:49
  7.9 98.7 %all-gather.7.cloned.1.call-start = ((), (), s32[]{:S(2)}) async-start(), calls=%async_computation.2 | async-start | bytes 6684672 | tf_op jit(solution)/shard_map/all_gather | solution.py:50
  8.7 469.8 %all-gather.9.cloned.1.call-start = ((), (), s32[]{:S(2)}) async-start(), calls=%async_computation.3 | async-start | bytes 6684672 | tf_op jit(solution)/shard_map/all_gather | solution.py:68
  413.7 86.7 %all-gather.11.cloned.1.call-start = ((), (), s32[]{:S(2)}) async-start(), calls=%async_computation.4 | async-start | bytes 7077888 | tf_op jit(solution)/shard_map/all_gather | solution.py:72
  414.3 200.0 %reduce-scatter.2.cloned.1.call-start = ((), (), s32[]{:S(2)}) async-start(), calls=%async_computation.5 | async-start | bytes 10027008 | tf_op jit(solution)/shard_map/reduce_scatter | solution.py:76
Sparse Core Ops, SparseCore 0:
  9.8 50.2 all-gather.4
  62.0 44.6 all-gather.6
  413.9 64.5 all-gather.8
  480.1 20.2 all-gather.10
  502.8 111.4 reduce-scatter.1
where the time goes:
time: 627 us; the launch traced here: 623 us
  waiting for transfers between devices  278 us (44%)
  matrix products  115 us (18%)
  local copies, waits for them, and re-layouts  110 us (18%)
  other arithmetic  75.8 us (12%)
  loops' own time  29.9 us (5%)
  between operations  13.8 us (2%)
    reduce_scatter x1, waiting for transfers between devices, body(): lax.psum_scatter(lax.dot_general(head_columns, cotangent, (((0,), (0,)),...  106 us
    dynamic_slice x64, local copies, waits for them, and re-layouts, body(): lax.scan(one_block, start_state, (key_stack, value_stack, block_columns))  96.5 us
    all_gather x1, waiting for transfers between devices, body(): all_heads = lax.all_gather(attended, 'row', axis=1, tiled=True)  64.1 us
    dot_general x16, matrix products, attend_block(): jnp.einsum('thu,uhd->thd', weights.astype(jnp.bfloat16), value_heads, pre...  58.4 us
    all_gather x1, waiting for transfers between devices, body(): key_piece = lax.all_gather(keys, ('col', 'ctx'), axis=0, tiled=True)  48.1 us
    all_gather x1, waiting for transfers between devices, body(): value_piece = lax.all_gather(values, ('col', 'ctx'), axis=0, tiled=True)  46.5 us
    dot_general x16, matrix products, attend_block(): jnp.einsum('thd,uhd->thu', query_heads, key_heads, preferred_element_type...  38.2 us
    another operation x1, loops' own time, body(): lax.scan(one_block, start_state, (key_stack, value_stack, block_columns))  29.9 us
  transfers between devices with their start and end apart: 5, of which 5 were waited for; matrix products, arithmetic and copies ran while one was open for 3% of the time, Pallas kernels for 0%

commit v1 on v0

--- a/solution.py
+++ b/solution.py
@@ -7,6 +7,22 @@
 HD = 128
 BLOCK = 512
 NEGATIVE_FILL = -1e30
+
+
+def gather_around(x, axis, dim):
+    ways, here, hop = (lax.axis_size(axis), lax.axis_index(axis), x.shape[dim])
+    shape = [n * ways if d == dim else n for d, n in enumerate(x.shape)]
+    full = lax.dynamic_update_slice_in_dim(jnp.zeros(shape, x.dtype), x, here * hop, axis=dim)
+    going_up = going_down = x
+    for far in range(1, ways // 2 + 1):
+        going_up = lax.ppermute(going_up, axis, [(d, (d + 1) % ways) for d in range(ways)])
+        full = lax.dynamic_update_slice_in_dim(full, going_up, (here - far) % ways * hop, axis=dim)
+        if 2 * far < ways:
+            going_down = lax.ppermute(going_down, axis, [(d, (d - 1) % ways) for d in range(ways)])
+            full = lax.dynamic_update_slice_in_dim(
+                full, going_down, (here + far) % ways * hop, axis=dim
+            )
+    return full
 
 
 def attend_block(carried, query_heads, key_block, value_block, allowed, score_scale):
@@ -46,7 +62,7 @@
         jnp.zeros((tok_rows, head_count), jnp.float32),
         jnp.zeros((tok_rows, head_count, HD), jnp.float32),
     )
-    key_piece = lax.all_gather(keys, ("col", "ctx"), axis=0, tiled=True)
+    key_piece = gather_around(keys, ("col", "ctx"), 0)
     value_piece = lax.all_gather(values, ("col", "ctx"), axis=0, tiled=True)
     block_count = key_piece.shape[0] // BLOCK
     key_stack = key_piece.reshape(block_count, BLOCK, feature_width)

time: 627 us -> 650 us (1.037)
  starting transfers between devices: 0.19 us -> 27.4 us
  waiting for transfers between devices: 278 us -> 257 us
  local copies, waits for them, and re-layouts: 110 us -> 127 us
    ppermute x0 -> x15, waiting for transfers between devices: none -> 76.4 us  [the longest x8 60.5 us: gather_around(): lax.ppermute(going_up, axis, [(d, (d + 1) % ways) for d in range(ways)])]
    all_gather x1 -> x0, waiting for transfers between devices: 48.1 us -> none  [body(): key_piece = lax.all_gather(keys, ('col', 'ctx'), axis=0, tiled=True)]
    all_gather x1, waiting for transfers between devices: 46.5 us -> 0.01 us  [body(): value_piece = lax.all_gather(values, ('col', 'ctx'), axis=0, tiled=True)]
    ppermute x0 -> x15, starting transfers between devices: none -> 27.3 us  [the longest x7 24.7 us: gather_around(): lax.ppermute(going_down, axis, [(d, (d - 1) % ways) for d in range(ways)])]
    dynamic_update_slice x0 -> x16, local copies, waits for them, and re-layouts: none -> 13.7 us  [the longest x8 7.38 us: gather_around(): lax.dynamic_update_slice_in_dim(full, going_up, (here - far) % ways * hop...]
  transfers between devices with their start and end apart: 5 -> 19, of which waited for: 5 -> 12; matrix products, arithmetic and copies ran while one was open for 3% -> 6% of each run, Pallas kernels for 0% -> 0%
where the time goes in v1:
time: 650 us; the launch traced here: 646 us
  waiting for transfers between devices  257 us (40%)
  local copies, waits for them, and re-layouts  127 us (20%)
  matrix products  114 us (18%)
  other arithmetic  74.8 us (12%)
  loops' own time  31.4 us (5%)
  starting transfers between devices  27.4 us (4%)
  between operations  13.8 us (2%)
    reduce_scatter x1, waiting for transfers between devices, body(): lax.psum_scatter(lax.dot_general(head_columns, cotangent, (((0,), (0,)),...  106 us
    dynamic_slice x64, local copies, waits for them, and re-layouts, body(): lax.scan(one_block, start_state, (key_stack, value_stack, block_columns))  97.1 us
    all_gather x1, waiting for transfers between devices, body(): all_heads = lax.all_gather(attended, 'row', axis=1, tiled=True)  61.6 us
    ppermute x8, waiting for transfers between devices, gather_around(): lax.ppermute(going_up, axis, [(d, (d + 1) % ways) for d in range(ways)])  60.5 us
    dot_general x16, matrix products, attend_block(): jnp.einsum('thu,uhd->thd', weights.astype(jnp.bfloat16), value_heads, pre...  57.9 us
    dot_general x16, matrix products, attend_block(): jnp.einsum('thd,uhd->thu', query_heads, key_heads, preferred_element_type...  37.4 us
    another operation x1, loops' own time, body(): lax.scan(one_block, start_state, (key_stack, value_stack, block_columns))  31.4 us
    ppermute x7, starting transfers between devices, gather_around(): lax.ppermute(going_down, axis, [(d, (d - 1) % ways) for d in range(ways)])  24.7 us
  transfers between devices with their start and end apart: 19, of which 12 were waited for; matrix products, arithmetic and copies ran while one was open for 6% of the time, Pallas kernels for 0%

profile of v1, /device:TPU:1, one launch (start us, length us, event | category | flops | bytes accessed | tf_op | source)
XLA Modules:
  0.0 645.5 jit_solution(2379721795635148108)
XLA Ops:
  10.5 4.6 collective-permute-start.1
  15.1 8.9 %collective-permute-done = bf16[512,384]{1,0:T(8,128)(2,1)S(1)} collective-permute-done((bf16[512,384]{1,0:T(8,128)(2,1)}, bf16[512,384]{1,0:T(8,128)(2,1)S(1)}, u32[]{:S(2)}, u32[]{:S(2)}) %collective-permute-start) | collective-permute-done | bytes 393248 | tf_op jit(solution)/shard_map/ppermute | solution.py:18
  24.4 3.6 collective-permute-start.3
  27.9 16.4 %collective-permute-done.2 = bf16[512,384]{1,0:T(8,128)(2,1)S(1)} collective-permute-done((bf16[512,384]{1,0:T(8,128)(2,1)S(1)}, bf16[512,384]{1,0:T(8,128)(2,1)S(1)}, u32[]{:S(2)}, u32[]{:S(2)}) %collective-permute-start.2) | collective-permute-done | bytes 393248 | tf_op jit(solution)/shard_map/ppermute | solution.py:18
  47.3 17.5 %collective-permute-done.4 = bf16[512,384]{1,0:T(8,128)(2,1)S(1)} collective-permute-done((bf16[512,384]{1,0:T(8,128)(2,1)S(1)}, bf16[512,384]{1,0:T(8,128)(2,1)S(1)}, u32[]{:S(2)}, u32[]{:S(2)}) %collective-permute-start.4) | collective-permute-done | bytes 393248 | tf_op jit(solution)/shard_map/ppermute | solution.py:18
  68.0 14.1 %collective-permute-done.6 = bf16[512,384]{1,0:T(8,128)(2,1)S(1)} collective-permute-done((bf16[512,384]{1,0:T(8,128)(2,1)S(1)}, bf16[512,384]{1,0:T(8,128)(2,1)S(1)}, u32[]{:S(2)}, u32[]{:S(2)}) %collective-permute-start.6) | collective-permute-done | bytes 393248 | tf_op jit(solution)/shard_map/ppermute | solution.py:18
  96.5 5.5 collective-permute-done.9
  101.9 3.7 collective-permute-start.11
  109.8 4.6 collective-permute-done.11
  114.5 3.7 collective-permute-start.13
  121.3 5.5 collective-permute-done.13
  132.5 304.3 %while.22 = (s32[]{:T(128)}, f32[512,3]{0,1:T(4,128)}, f32[512,3]{0,1:T(4,128)}, f32[512,3,128]{0,2,1:T(8,128)}, s32[16]{0:T(128)}, /*index=5*/s32[1,16]{1,0:T(1...) while((s32[]{:T(128)}, f32[512,3]{0,1:T(4,128)}, ...), condition=%wide.region_3.4_spmd.clone, body=%wide.region_0.3_spmd.clone.sunk | while | flops 413474304 | bytes 15433919 | solution.py:79
  164.8 3.6 fusion.42
  184.0 3.6 fusion.42
  203.1 3.6 fusion.42
  222.2 3.6 fusion.42
  241.3 3.6 fusion.42
  260.5 3.6 fusion.42
  279.6 3.6 fusion.42
  298.7 3.6 fusion.42
  317.8 3.6 fusion.42
  337.0 3.6 fusion.42
  356.1 3.6 fusion.42
  375.2 3.6 fusion.42
  394.3 3.6 fusion.42
  413.5 3.6 fusion.42
  432.6 3.6 fusion.42
  439.6 61.6 %all-gather.6.cloned.1.call-done = bf16[512,6144]{0,1:T(8,128)(2,1)} async-done(((bf16[512,384]{0,1:T(8,128)(2,1)}), bf16[512,6144]{0,1:T(8,128)(2,1)}) %all-gather.6.cloned.1.call-update) | async-done | bytes 6291472 | tf_op jit(solution)/shard_map/all_gather | solution.py:84
  501.2 9.9 %fusion.19 = f32[6144,384]{1,0:T(8,128)} fusion(bf16[512,6144]{0,1:T(8,128)(2,1)} %all-gather.6.cloned.1.call-done, bf16[512,384]{1,0:T(8,128)(2,1)S(1)} %copy-done), kind=kOutput, calls=%fused_computation.43 | convolution fusion | flops 2415919104 | bytes 16121856 | tf_op jit(solution)/shard_map/dot_general | solution.py:93
  511.1 12.2 %all-gather.8.cloned.1.call-done = bf16[6144,384]{1,0:T(8,128)(2,1)} async-done(((bf16[3072,384]{1,0:T(8,128)(2,1)}), bf16[6144,384]{1,0:T(8,128)(2,1)}) %all-gather.8.cloned.1.call-update) | async-done | bytes 4718608 | tf_op jit(solution)/shard_map/all_gather | solution.py:88
  523.3 8.3 %convolution_convert_fusion = bf16[512,384]{1,0:T(8,128)(2,1)} fusion(bf16[512,6144]{0,1:T(8,128)(2,1)} %all-gather.6.cloned.1.call-done, bf16[6144,384]{1,0:T(8,128)(2,1)} %all-gather.8.cloned.1.call-done), kind=kOutput, calls=%fused_computation.23 | convolution fusion | flops 2416115712 | bytes 11403264 | tf_op jit(solution)/shard_map/dot_general | solution.py:86
  531.6 105.5 %reduce-scatter.2.cloned.1.call-done = f32[384,384]{1,0:T(8,128)} async-done(((f32[6144,384]{1,0:T(8,128)}), f32[384,384]{1,0:T(8,128)}) %reduce-scatter.2.cloned.1.call-update) | async-done | bytes 589840 | tf_op jit(solution)/shard_map/reduce_scatter | solution.py:92
  (227 shorter events, 260.1 us)
Async XLA Ops:
  7.2 494.1 %copy-start = (bf16[512,384]{1,0:T(8,128)(2,1)S(1)}, bf16[512,384]{1,0:T(8,128)(2,1)}, u32[]{:S(2)}) copy-start(bf16[512,384]{1,0:T(8,128)(2,1)} %param.16) | copy-start | bytes 1179652
  7.2 81.5 %copy-start.1 = (bf16[512,384]{1,0:T(8,128)(2,1)S(1)}, bf16[512,384]{1,0:T(8,128)(2,1)}, u32[]{:S(2)}) copy-start(bf16[512,384]{1,0:T(8,128)(2,1)} %param.13) | copy-start | bytes 1179652
  7.2 124.7 %all-gather.4.cloned.1.call-start = ((), (), s32[]{:S(2)}) async-start(), calls=%async_computation.1 | async-start | bytes 6684672 | tf_op jit(solution)/shard_map/all_gather | solution.py:66
  7.9 493.3 %all-gather.6.cloned.1.call-start = ((), (), s32[]{:S(2)}) async-start(), calls=%async_computation.2 | async-start | bytes 6684672 | tf_op jit(solution)/shard_map/all_gather | solution.py:84
  8.0 16.1 %collective-permute-start = (bf16[512,384]{1,0:T(8,128)(2,1)}, bf16[512,384]{1,0:T(8,128)(2,1)S(1)}, u32[]{:S(2)}, u32[]{:S(2)}) collective-permute-start(bf16[512,384]{1,0:T(8,128)(2,1)} %param.13), channel_id=1, source_target_pairs={{0,1},{1,2},{2,3},{3,4},{4,5},{5,6},{6,7},{7,8},{8,9},{9,10},{10,1... | collective-permute-start | bytes 1179656 | tf_op jit(solution)/shard_map/ppermute | solution.py:18
  10.5 13.8 %collective-permute-start.1 = (bf16[512,384]{1,0:T(8,128)(2,1)}, bf16[512,384]{1,0:T(8,128)(2,1)S(1)}, u32[]{:S(2)}, u32[]{:S(2)}) collective-permute-start(bf16[512,384]{1,0:T(8,128)(2,1)} %param.13), channel_id=1, source_target_pairs={{0,15},{1,0},{2,1},{3,2},{4,3},{5,4},{6,5},{7,6},{8,7},{9,8},{10,9... | collective-permute-start | bytes 1179656 | tf_op jit(solution)/shard_map/ppermute | solution.py:21
  24.1 23.3 %copy-start.4 = (bf16[512,384]{1,0:T(8,128)(2,1)}, bf16[512,384]{1,0:T(8,128)(2,1)S(1)}, u32[]{:S(2)}) copy-start(bf16[512,384]{1,0:T(8,128)(2,1)S(1)} %collective-permute-done) | copy-start | bytes 1179652
  24.1 20.3 %collective-permute-start.2 = (bf16[512,384]{1,0:T(8,128)(2,1)S(1)}, bf16[512,384]{1,0:T(8,128)(2,1)S(1)}, u32[]{:S(2)}, u32[]{:S(2)}) collective-permute-start(bf16[512,384]{1,0:T(8,128)(2,1)S(1)} %collective-permute-done), channel_id=1, source_target_pairs={{0,1},{1,2},{2,3},{3,4},{4,5},{5,6},{6,7},{7,8},{8,9},{9,10},{10,1... | collective-permute-start | bytes 1179656 | tf_op jit(solution)/shard_map/ppermute | solution.py:18
  24.4 20.0 %collective-permute-start.3 = (bf16[512,384]{1,0:T(8,128)(2,1)S(1)}, bf16[512,384]{1,0:T(8,128)(2,1)S(1)}, u32[]{:S(2)}, u32[]{:S(2)}) collective-permute-start(bf16[512,384]{1,0:T(8,128)(2,1)S(1)} %collective-permute-done.1), channel_id=1, source_target_pairs={{0,15},{1,0},{2,1},{3,2},{4,3},{5,4},{6,5},{7,6},{8,7},{9,8},{10,9... | collective-permute-start | bytes 1179656 | tf_op jit(solution)/shard_map/ppermute | solution.py:21
  44.4 20.5 %collective-permute-start.4 = (bf16[512,384]{1,0:T(8,128)(2,1)S(1)}, bf16[512,384]{1,0:T(8,128)(2,1)S(1)}, u32[]{:S(2)}, u32[]{:S(2)}) collective-permute-start(bf16[512,384]{1,0:T(8,128)(2,1)S(1)} %collective-permute-done.2), channel_id=1, source_target_pairs={{0,1},{1,2},{2,3},{3,4},{4,5},{5,6},{6,7},{7,8},{8,9},{9,10},{10,1... | collective-permute-start | bytes 1179656 | tf_op jit(solution)/shard_map/ppermute | solution.py:18
  44.4 20.5 %collective-permute-start.5 = (bf16[512,384]{1,0:T(8,128)(2,1)S(1)}, bf16[512,384]{1,0:T(8,128)(2,1)S(1)}, u32[]{:S(2)}, u32[]{:S(2)}) collective-permute-start(bf16[512,384]{1,0:T(8,128)(2,1)S(1)} %collective-permute-done.3), channel_id=1, source_target_pairs={{0,15},{1,0},{2,1},{3,2},{4,3},{5,4},{6,5},{7,6},{8,7},{9,8},{10,9... | collective-permute-start | bytes 1179656 | tf_op jit(solution)/shard_map/ppermute | solution.py:21
  64.8 18.6 %copy-start.2 = (bf16[512,384]{1,0:T(8,128)(2,1)}, bf16[512,384]{1,0:T(8,128)(2,1)S(1)}, u32[]{:S(2)}) copy-start(bf16[512,384]{1,0:T(8,128)(2,1)S(1)} %collective-permute-done.4) | copy-start | bytes 1179652
  64.8 17.4 %collective-permute-start.6 = (bf16[512,384]{1,0:T(8,128)(2,1)S(1)}, bf16[512,384]{1,0:T(8,128)(2,1)S(1)}, u32[]{:S(2)}, u32[]{:S(2)}) collective-permute-start(bf16[512,384]{1,0:T(8,128)(2,1)S(1)} %collective-permute-done.4), channel_id=1, source_target_pairs={{0,1},{1,2},{2,3},{3,4},{4,5},{5,6},{6,7},{7,8},{8,9},{9,10},{10,1... | collective-permute-start | bytes 1179656 | tf_op jit(solution)/shard_map/ppermute | solution.py:18
  64.8 25.4 %collective-permute-start.7 = (bf16[512,384]{1,0:T(8,128)(2,1)S(1)}, bf16[512,384]{1,0:T(8,128)(2,1)S(1)}, u32[]{:S(2)}, u32[]{:S(2)}) collective-permute-start(bf16[512,384]{1,0:T(8,128)(2,1)S(1)} %collective-permute-done.5), channel_id=1, source_target_pairs={{0,15},{1,0},{2,1},{3,2},{4,3},{5,4},{6,5},{7,6},{8,7},{9,8},{10,9... | collective-permute-start | bytes 1179656 | tf_op jit(solution)/shard_map/ppermute | solution.py:21
  82.2 11.8 %collective-permute-start.8 = (bf16[512,384]{1,0:T(8,128)(2,1)S(1)}, bf16[512,384]{1,0:T(8,128)(2,1)}, u32[]{:S(2)}, u32[]{:S(2)}) collective-permute-start(bf16[512,384]{1,0:T(8,128)(2,1)S(1)} %collective-permute-done.6), channel_id=1, source_target_pairs={{0,1},{1,2},{2,3},{3,4},{4,5},{5,6},{6,7},{7,8},{8,9},{9,10},{10,1... | collective-permute-start | bytes 1179656 | tf_op jit(solution)/shard_map/ppermute | solution.py:18
  85.5 10.1 %copy-start.3 = (bf16[512,384]{1,0:T(8,128)(2,1)S(1)}, bf16[512,384]{1,0:T(8,128)(2,1)}, u32[]{:S(2)}) copy-start(bf16[512,384]{1,0:T(8,128)(2,1)} %copy-done.2) | copy-start | bytes 1179652
  85.5 4.0 copy-start.5
  90.3 11.7 %collective-permute-start.9 = (bf16[512,384]{1,0:T(8,128)(2,1)S(1)}, bf16[512,384]{1,0:T(8,128)(2,1)S(1)}, u32[]{:S(2)}, u32[]{:S(2)}) collective-permute-start(bf16[512,384]{1,0:T(8,128)(2,1)S(1)} %collective-permute-done.7), channel_id=1, source_target_pairs={{0,15},{1,0},{2,1},{3,2},{4,3},{5,4},{6,5},{7,6},{8,7},{9,8},{10,9... | collective-permute-start | bytes 1179656 | tf_op jit(solution)/shard_map/ppermute | solution.py:21
  94.0 12.4 %collective-permute-start.10 = (bf16[512,384]{1,0:T(8,128)(2,1)}, bf16[512,384]{1,0:T(8,128)(2,1)S(1)}, u32[]{:S(2)}, u32[]{:S(2)}) collective-permute-start(bf16[512,384]{1,0:T(8,128)(2,1)} %collective-permute-done.8), channel_id=1, source_target_pairs={{0,1},{1,2},{2,3},{3,4},{4,5},{5,6},{6,7},{7,8},{8,9},{9,10},{10,1... | collective-permute-start | bytes 1179656 | tf_op jit(solution)/shard_map/ppermute | solution.py:18
  101.9 12.5 %collective-permute-start.11 = (bf16[512,384]{1,0:T(8,128)(2,1)S(1)}, bf16[512,384]{1,0:T(8,128)(2,1)S(1)}, u32[]{:S(2)}, u32[]{:S(2)}) collective-permute-start(bf16[512,384]{1,0:T(8,128)(2,1)S(1)} %collective-permute-done.9), channel_id=1, source_target_pairs={{0,15},{1,0},{2,1},{3,2},{4,3},{5,4},{6,5},{7,6},{8,7},{9,8},{10,9... | collective-permute-start | bytes 1179656 | tf_op jit(solution)/shard_map/ppermute | solution.py:21
  106.4 12.5 %collective-permute-start.12 = (bf16[512,384]{1,0:T(8,128)(2,1)S(1)}, bf16[512,384]{1,0:T(8,128)(2,1)S(1)}, u32[]{:S(2)}, u32[]{:S(2)}) collective-permute-start(bf16[512,384]{1,0:T(8,128)(2,1)S(1)} %collective-permute-done.10), channel_id=1, source_target_pairs={{0,1},{1,2},{2,3},{3,4},{4,5},{5,6},{6,7},{7,8},{8,9},{9,10},{10,1... | collective-permute-start | bytes 1179656 | tf_op jit(solution)/shard_map/ppermute | solution.py:18
  114.5 12.3 %collective-permute-start.13 = (bf16[512,384]{1,0:T(8,128)(2,1)S(1)}, bf16[512,384]{1,0:T(8,128)(2,1)S(1)}, u32[]{:S(2)}, u32[]{:S(2)}) collective-permute-start(bf16[512,384]{1,0:T(8,128)(2,1)S(1)} %collective-permute-done.11), channel_id=1, source_target_pairs={{0,15},{1,0},{2,1},{3,2},{4,3},{5,4},{6,5},{7,6},{8,7},{9,8},{10,9... | collective-permute-start | bytes 1179656 | tf_op jit(solution)/shard_map/ppermute | solution.py:21
  119.0 12.1 %collective-permute-start.14 = (bf16[512,384]{1,0:T(8,128)(2,1)S(1)}, bf16[512,384]{1,0:T(8,128)(2,1)S(1)}, u32[]{:S(2)}, u32[]{:S(2)}) collective-permute-start(bf16[512,384]{1,0:T(8,128)(2,1)S(1)} %collective-permute-done.12), channel_id=1, source_target_pairs={{0,1},{1,2},{2,3},{3,4},{4,5},{5,6},{6,7},{7,8},{8,9},{9,10},{10,1... | collective-permute-start | bytes 1179656 | tf_op jit(solution)/shard_map/ppermute | solution.py:18
  438.8 84.5 %all-gather.8.cloned.1.call-start = ((), (), s32[]{:S(2)}) async-start(), calls=%async_computation.3 | async-start | bytes 7077888 | tf_op jit(solution)/shard_map/all_gather | solution.py:88
  439.5 197.6 %reduce-scatter.2.cloned.1.call-start = ((), (), s32[]{:S(2)}) async-start(), calls=%async_computation.4 | async-start | bytes 10027008 | tf_op jit(solution)/shard_map/reduce_scatter | solution.py:92
Sparse Core Ops, SparseCore 0:
  9.9 72.8 all-gather.3
  438.9 62.2 all-gather.5
  503.0 20.2 all-gather.7
  525.7 111.4 reduce-scatter.1
